TPU v7x, 32 devices: a whole 2x2x4 slice. The times are simulated.
32 devices in a mesh: ctx: 8 (over y, x, core), head: 4 (over z).
Axes of the slice: x: 2, y: 2, z: 4, core: 2. Of those that a mesh axis runs over, the one named last changes fastest.
Arguments:
- query_input: bfloat16 [8, 512, 4096], P('ctx', 'head'), may hold values from -6 to 6
- key_input: bfloat16 [8, 512, 512], P('ctx', 'head'), may hold values from -6 to 6
- value_input: bfloat16 [8, 512, 512], P('ctx', 'head'), may hold values from -6 to 6
- grad_input: bfloat16 [8, 512, 4096], P('ctx', 'head'), may hold values from -6 to 6
Outputs:
- attended: bfloat16 [8, 512, 4096], P('ctx', 'head')
- query_grad: float32 [8, 512, 4096], P('ctx', 'head')
- key_grad: float32 [8, 512, 512], P('ctx', 'head')
- value_grad: float32 [8, 512, 512], P('ctx', 'head')
All inputs are finite; a program needn't handle non-finite values.
Results may differ from a plain program's by a relative error of at most 0.0076.
Values may be sent and summed in bfloat16 or wider, within the bound.
A program may use at most 192 MiB of HBM per device.

v0:
```python
import math

import jax
import jax.numpy as jnp
from jax import lax
from jax.sharding import PartitionSpec as P

HD = 128


def from_partner(value, axis, apart):
    mask = 2**apart
    pairs = [(source, source ^ mask) for source in range(lax.axis_size(axis))]
    return lax.ppermute(value, axis, pairs)


def attend(query_split, grad_split, query_pos, key_all, value_all, key_span, scaling):
    rows, pair_heads, sharing, head_dim = query_split.shape
    block_total = (jnp.max(query_pos) + key_span) // key_span

    def block_scores(begin_row):
        key_block = lax.dynamic_slice_in_dim(key_all, begin_row, key_span, 0).reshape(
            key_span, pair_heads, head_dim
        )
        raw_scores = (
            jnp.einsum("ihgd,jhd->hgij", query_split, key_block, preferred_element_type=jnp.float32)
            * scaling
        )
        allowed = (begin_row + jnp.arange(key_span, dtype=jnp.int32))[None, :] <= query_pos[:, None]
        return (jnp.where(allowed, raw_scores, -jnp.inf), key_block)

    def value_slice(begin_row):
        return lax.dynamic_slice_in_dim(value_all, begin_row, key_span, 0).reshape(
            key_span, pair_heads, head_dim
        )

    def stats_pass(step_num, state_in):
        running_max, running_sum = state_in
        scores, unused = block_scores(step_num * key_span)
        highest = jnp.maximum(running_max, jnp.max(scores, axis=-1))
        rescale = jnp.exp(running_max - highest)
        running_sum = running_sum * rescale + jnp.sum(jnp.exp(scores - highest[..., None]), axis=-1)
        return (highest, running_sum)

    stat_shape = (pair_heads, sharing, rows)
    highest, running_sum = lax.fori_loop(
        0,
        block_total,
        stats_pass,
        (jnp.full(stat_shape, -jnp.inf, jnp.float32), jnp.zeros(stat_shape, jnp.float32)),
    )
    log_total = highest + jnp.log(running_sum)

    def output_pass(step_num, running_out):
        begin_row = step_num * key_span
        scores, unused = block_scores(begin_row)
        weights = jnp.exp(scores - log_total[..., None]).astype(jnp.bfloat16)
        return running_out + jnp.einsum(
            "hgij,jhd->hgid", weights, value_slice(begin_row), preferred_element_type=jnp.float32
        )

    running_out = lax.fori_loop(
        0, block_total, output_pass, jnp.zeros(stat_shape + (head_dim,), jnp.float32)
    )
    attended = running_out.transpose(2, 0, 1, 3).astype(jnp.bfloat16)
    row_dot = jnp.sum(
        grad_split.astype(jnp.float32) * attended.astype(jnp.float32), axis=-1
    ).transpose(1, 2, 0)

    def grad_pass(step_num, state_in):
        begin_row = step_num * key_span
        scores, key_block = block_scores(begin_row)
        value_block = value_slice(begin_row)
        normalized = jnp.exp(scores - log_total[..., None])
        weights = normalized.astype(jnp.bfloat16)
        weight_grad = jnp.einsum(
            "ihgd,jhd->hgij", grad_split, value_block, preferred_element_type=jnp.float32
        )
        score_grad = (normalized * (weight_grad - row_dot[..., None])).astype(jnp.bfloat16)
        query_sum = state_in[0] + jnp.einsum(
            "hgij,jhd->ihgd", score_grad, key_block, preferred_element_type=jnp.float32
        )
        return (query_sum,)

    query_zero = jnp.zeros((rows, pair_heads, sharing, head_dim), jnp.float32)
    initial = (query_zero,)
    gradients = lax.fori_loop(0, block_total, grad_pass, initial)
    sums_out = None
    return (attended, gradients[0], sums_out, log_total, row_dot)


def on_device(query_input, key_input, value_input, grad_input):
    local_rows = query_input.shape[1]
    query_width = query_input.shape[2]
    pair_width = key_input.shape[2]
    pair_heads = pair_width // HD
    sharing = query_width // pair_width
    local_heads = pair_heads * sharing
    block_count = lax.axis_size("ctx")
    block_rows = 2 * local_rows
    all_rows = block_count * block_rows
    key_span = min(512, all_rows)
    scaling = 1.0 / math.sqrt(HD)
    block_index = lax.axis_index("ctx")
    half_index = lax.axis_index("head") % 2
    block_first = block_index * block_rows
    first_row = block_first + half_index * local_rows
    query_local = query_input.reshape(local_rows, query_width)
    grad_local = grad_input.reshape(local_rows, query_width)
    own_pairs = jnp.stack(
        [key_input.reshape(local_rows, pair_width), value_input.reshape(local_rows, pair_width)]
    )
    partner_pairs = from_partner(own_pairs, "head", 0)
    block_pairs = jnp.where(
        half_index == 0,
        jnp.concatenate([own_pairs, partner_pairs], axis=1),
        jnp.concatenate([partner_pairs, own_pairs], axis=1),
    )
    gathered_pairs = lax.all_gather(block_pairs, "ctx", axis=1, tiled=True)
    key_all = gathered_pairs[0]
    value_all = gathered_pairs[1]
    query_split = query_local.reshape(local_rows, pair_heads, sharing, HD)
    grad_split = grad_local.reshape(local_rows, pair_heads, sharing, HD)
    query_pos = first_row + jnp.arange(local_rows, dtype=jnp.int32)
    sums_in = None
    attended, query_sum, sums_out, log_total, row_dot = attend(
        query_split, grad_split, query_pos, key_all, value_all, key_span, scaling
    )
    query_grad = scaling * query_sum
    total_rows = log_total.reshape(local_heads, local_rows).T
    dot_rows = row_dot.reshape(local_heads, local_rows).T
    total_all, dot_all = (
        lax.all_gather(total_rows, "ctx", axis=0, tiled=True),
        lax.all_gather(dot_rows, "ctx", axis=0, tiled=True),
    )
    block_keys = block_pairs[0].reshape(block_rows, pair_heads, HD)
    block_values = block_pairs[1].reshape(block_rows, pair_heads, HD)
    key_pos = block_first + jnp.arange(block_rows, dtype=jnp.int32)
    zero_rows = jnp.zeros((block_rows, pair_width), jnp.float32)
    query_piece = lax.all_gather(query_local, "ctx", axis=0, tiled=True)
    grad_piece = lax.all_gather(grad_local, "ctx", axis=0, tiled=True)
    piece_rows = query_piece.shape[0]
    query_span = math.gcd(piece_rows, 512)
    span_total = piece_rows // query_span

    def one_block(step_num, sums_in):
        offset = step_num * query_span
        gathered_index = offset + jnp.arange(query_span, dtype=jnp.int32)
        row_pos = (
            gathered_index // local_rows * block_rows
            + half_index * local_rows
            + gathered_index % local_rows
        )

        def accumulate(sums_now):
            query_block = lax.dynamic_slice_in_dim(query_piece, offset, query_span, 0).reshape(
                query_span, pair_heads, sharing, HD
            )
            grad_block = lax.dynamic_slice_in_dim(grad_piece, offset, query_span, 0).reshape(
                query_span, pair_heads, sharing, HD
            )
            total_block = lax.dynamic_slice_in_dim(total_all, offset, query_span, 0).T.reshape(
                pair_heads, sharing, query_span
            )
            dot_block = lax.dynamic_slice_in_dim(dot_all, offset, query_span, 0).T.reshape(
                pair_heads, sharing, query_span
            )
            raw_scores = (
                jnp.einsum(
                    "ihgd,jhd->hgij", query_block, block_keys, preferred_element_type=jnp.float32
                )
                * scaling
            )
            allowed = key_pos[None, :] <= row_pos[:, None]
            normalized = jnp.exp(jnp.where(allowed, raw_scores, -jnp.inf) - total_block[..., None])
            weights = normalized.astype(jnp.bfloat16)
            weight_grad = jnp.einsum(
                "ihgd,jhd->hgij", grad_block, block_values, preferred_element_type=jnp.float32
            )
            score_grad = (normalized * (weight_grad - dot_block[..., None])).astype(jnp.bfloat16)
            key_add = jnp.einsum(
                "hgij,ihgd->jhd", score_grad, query_block, preferred_element_type=jnp.float32
            ).reshape(block_rows, pair_width)
            value_add = jnp.einsum(
                "hgij,ihgd->jhd", weights, grad_block, preferred_element_type=jnp.float32
            ).reshape(block_rows, pair_width)
            return (sums_now[0] + key_add, sums_now[1] + value_add)

        def unchanged(sums_now):
            return sums_now

        return lax.cond(jnp.max(row_pos) >= block_first, accumulate, unchanged, sums_in)

    key_sum, value_sum = lax.fori_loop(0, span_total, one_block, (zero_rows, zero_rows))
    outgoing = jnp.stack(
        [
            lax.dynamic_slice_in_dim(key_sum, (1 - half_index) * local_rows, local_rows, 0),
            lax.dynamic_slice_in_dim(value_sum, (1 - half_index) * local_rows, local_rows, 0),
        ]
    )
    incoming = from_partner(outgoing.astype(jnp.bfloat16), "head", 0).astype(outgoing.dtype)
    key_mine = (
        lax.dynamic_slice_in_dim(key_sum, half_index * local_rows, local_rows, 0) + incoming[0]
    )
    value_mine = (
        lax.dynamic_slice_in_dim(value_sum, half_index * local_rows, local_rows, 0) + incoming[1]
    )
    key_grad = scaling * key_mine
    return (
        attended.reshape(1, local_rows, query_width),
        query_grad.reshape(1, local_rows, query_width),
        key_grad.reshape(1, local_rows, pair_width),
        value_mine.reshape(1, local_rows, pair_width),
    )


def solution(mesh):
    in_specs = (
        P("ctx", "head", None),
        P("ctx", "head", None),
        P("ctx", "head", None),
        P("ctx", "head", None),
    )
    out_specs = (
        P("ctx", "head", None),
        P("ctx", "head", None),
        P("ctx", "head", None),
        P("ctx", "head", None),
    )
    return jax.shard_map(
        on_device, mesh=mesh, in_specs=in_specs, out_specs=out_specs, check_vma=False
    )
```

profile of v0, /device:TPU:0, one launch (start us, length us, event | category | flops | bytes accessed | tf_op | source)
XLA Modules:
  0.0 268.0 jit_solution(2560480895931891677)
XLA Ops:
  9.0 3.1 %collective-permute-start = (bf16[2,128,512]{2,1,0:T(8,128)(2,1)S(1)}, bf16[2,128,512]{2,1,0:T(8,128)(2,1)S(1)}, u32[]{:S(2)}, u32[]{:S(2)}) collective-permute-start(bf16[2,128,512]{2,1,0:T(8,128)(2,1)S(1)} %constant_dynamic-update-slice_fusion), channel_id=1, source_target_pairs={{0,1},{1,0},{2,3},{3,2},{4,5},{5,4},{6,7},{7,6},{8,9},{9,8},{10,11... | collective-permute-start | bytes 786440 | tf_op jit(solution)/shard_map/ppermute | solution.py:14
  12.2 6.3 %collective-permute-done = bf16[2,128,512]{2,1,0:T(8,128)(2,1)S(1)} collective-permute-done((bf16[2,128,512]{2,1,0:T(8,128)(2,1)S(1)}, bf16[2,128,512]{2,1,0:T(8,128)(2,1)S(1)}, u32[]{:S(2)}, u32[]{:S(2)}) %collective-permute-start) | collective-permute-done | bytes 262176 | tf_op jit(solution)/shard_map/ppermute | solution.py:14
  19.6 2.3 copy.67
  27.2 2.3 copy.79
  30.7 26.9 %all-gather.6.cloned.1.call-done = bf16[2,2048,512]{2,1,0:T(8,128)(2,1)} async-done(((bf16[2,256,512]{2,1,0:T(8,128)(2,1)}), bf16[2,2048,512]{2,1,0:T(8,128)(2,1)}) %all-gather.6.cloned.1.call-update) | async-done | bytes 4194320 | tf_op jit(solution)/shard_map/all_gather | solution.py:119
  57.7 3.8 %slice_bitcast_fusion = (bf16[2048,512]{1,0:T(8,128)(2,1)S(1)}, bf16[2048,512]{1,0:T(8,128)(2,1)}) fusion(bf16[2,2048,512]{2,1,0:T(8,128)(2,1)} %all-gather.6.cloned.1.call-done), kind=kLoop, calls=%fused_computation.84 | loop fusion | bytes 8388608 | tf_op jit(solution)/shard_map/squeeze | solution.py:121
  61.5 4.0 %copy.70 = bf16[2048,512]{0,1:T(8,128)(2,1)} copy(bf16[2048,512]{1,0:T(8,128)(2,1)} %get-tuple-element.818) | data formatting | bytes 4194304
  65.5 4.5 %while.54 = (s32[]{:T(128)}, f32[4,8,128]{2,1,0:T(8,128)S(1)}, f32[4,8,128]{2,1,0:T(8,128)S(1)}, s32[]{:T(128)}, bf16[2048,512]{0,1:T(8,128)(2,1)}, /*index=5*/b...) while((s32[]{:T(128)}, f32[4,8,128]{2,1,0:T(8,128)S(1)}, ...), condition=%wide.region_4.5_spmd.clone, body=%wide.region_1.4_spmd.clone.sunk | while | flops 551625344 | bytes 19813544 | solution.py:46
  70.0 2.4 copy.72
  74.0 7.7 %while.55 = (s32[]{:T(128)}, f32[4,8,128,128]{3,2,1,0:T(8,128)}, s32[]{:T(128)}, bf16[2048,512]{0,1:T(8,128)(2,1)}, bf16[128,4,8,128]{3,0,2,1:T(8,128)(2,1)S(1)}...) while((s32[]{:T(128)}, f32[4,8,128,128]{3,2,1,0:T(8,128)}, ...), condition=%wide.region_6.7_spmd.clone, body=%wide.region_5.6_spmd.clone.sunk | while | flops 1082720896 | bytes 8541359 | solution.py:62
  75.5 6.2 %fusion.106 = f32[4,8,128,128]{3,2,1,0:T(8,128)} fusion(f32[4,8,128,128]{3,2,1,0:T(8,128)} %get-tuple-element.1118, bf16[512,4,128,1]{0,2,3,1:T(8,128)(2,1)S(1)} %bitcast.232, f32[4,8,128]{2,1,0:T(8,128)S(1)} %get-tuple-element.1134, pred[128,512]{0,1:T(8,128)(4,1)S(1)} %broadcast_compare_fusion.8, bf16[512,4,128,1]{0,2,3,1:T(8,128)(2,1)S(1)} %bitcast.233, ...), kind=kOutput, calls=%fused_computation.46.clone.1 | convolution fusion | flops 1082654720 | bytes 6373376 | tf_op jit(solution)/shard_map/while/body/hgij,jhd->hgid/dot_general | solution.py:58
  81.8 2.6 copy.73
  88.8 45.8 %all_gather.17 = f32[1024,32]{0,1:T(8,128)S(1)} all-gather(f32[128,32]{0,1:T(8,128)S(1)} %bitcast.239), channel_id=1, replica_groups=mesh['ctx'=8,'head'=4] {'ctx'}, dimensions={0}, use_global_device_ids=true | all-gather | bytes 147456 | tf_op jit(solution)/shard_map/all_gather | solution.py:133
  134.6 10.2 %all_gather.19 = f32[1024,32]{0,1:T(8,128)S(1)} all-gather(f32[128,32]{0,1:T(8,128)S(1)} %bitcast.240), channel_id=1, replica_groups=mesh['ctx'=8,'head'=4] {'ctx'}, dimensions={0}, use_global_device_ids=true | all-gather | bytes 147456 | tf_op jit(solution)/shard_map/all_gather | solution.py:134
  146.3 14.6 %while.56 = (s32[]{:T(128)}, f32[128,4,8,128]{0,3,2,1:T(8,128)}, s32[]{:T(128)}, bf16[2048,512]{0,1:T(8,128)(2,1)}, bf16[128,4,8,128]{3,0,2,1:T(8,128)(2,1)S(1)}...) while((s32[]{:T(128)}, f32[128,4,8,128]{0,3,2,1:T(8,128)}, ...), condition=%wide.region_9.10_spmd.clone, body=%wide.region_8.9_spmd.clone.sunk | while | flops 1623786112 | bytes 26907840 | solution.py:87
  147.8 4.5 %fusion.113 = f32[4,512,128,8]{2,1,3,0:T(8,128)} fusion(bf16[512,4,128,1]{0,2,3,1:T(8,128)(2,1)S(1)} %bitcast.224, bf16[128,4,8,128]{3,0,2,1:T(8,128)(2,1)S(1)} %get-tuple-element.1173), kind=kOutput, calls=%fused_computation.106.clone.1 | convolution fusion | flops 536870912 | bytes 9961472 | tf_op jit(solution)/shard_map/while/body/ihgd,jhd->hgij/dot_general | solution.py:26
  152.3 8.6 %bitcast_add_fusion.4 = f32[128,4,8,128]{0,3,2,1:T(8,128)} fusion(f32[128,4,8,128]{0,3,2,1:T(8,128)} %get-tuple-element.1156, bf16[512,4,128,1]{0,2,3,1:T(8,128)(2,1)S(1)} %bitcast.225, f32[4,512,128,8]{2,1,3,0:T(8,128)} %fusion.113, f32[4,8,128]{2,1,0:T(8,128)S(1)} %get-tuple-element.1177, f32[4,8,128]{2,1,0:T(8,128)S(1)} %get-tuple-element.1174, ...), kind=kOutput, calls=%fused_computation.63.clone.1 | convolution fusion | flops 1086849024 | bytes 14778368 | tf_op jit(solution)/shard_map/while/body/hgij,jhd->ihgd/dot_general | solution.py:80
  161.0 12.8 %all-gather.10.cloned.1.call-done = bf16[1,1024,4096]{1,2,0:T(8,128)(2,1)} async-done(((bf16[1,128,4096]{1,2,0:T(8,128)(2,1)}), bf16[1,1024,4096]{1,2,0:T(8,128)(2,1)}) %all-gather.10.cloned.1.call-update) | async-done | bytes 8388624 | tf_op jit(solution)/shard_map/all_gather | solution.py:141
  173.8 76.9 %while.57 = (s32[]{:T(128)}, f32[256,512]{0,1:T(8,128)S(1)}, f32[256,512]{0,1:T(8,128)S(1)}, s32[]{:T(128)}, s32[]{:T(128)}, /*index=5*/bf16[1024,4096]{0,1:T(8,...) while((s32[]{:T(128)}, f32[256,512]{0,1:T(8,128)S(1)}, ...), condition=%wide.region_14.15_spmd.clone.clone, body=%wide.region_10.14_spmd.clone.clone.sunk | while | flops 4337315840 | bytes 139796880 | solution.py:194
  175.2 37.1 %conditional.4 = ((f32[256,512]{0,1:T(8,128)S(1)}, f32[256,512]{0,1:T(8,128)S(1)})) conditional(s32[]{:T(128)} %convert_element_type.67, (f32[256,512]{0,1:T(8,128)S(1)}, f32[256,512]{0,1:T(8,128)S(1)}) %tuple.139, (s32[]{:T(128)}, bf16[1024,4096]{0,1:T(8,128)(2,1)}, s32[]{:T(128)}, s32[512]{0:T(512)S(1)}, bf16[256,4,128]{2,0,1:T(8,128)(2,1)S(1)}, ...), branch_computations={%region_12.12_spmd, %region_13.13_spmd} | conditional | flops 4337303552 | bytes 139793536 | solution.py:192
  175.4 2.6 constant_dynamic-slice_fusion.1
  179.8 2.9 %constant_dynamic-slice_fusion = bf16[512,4096]{0,1:T(8,128)(2,1)} fusion(bf16[1024,4096]{0,1:T(8,128)(2,1)S(1)} %copy-done.1, s32[]{:T(128)S(6)} %select_n.81), kind=kLoop, calls=%fused_computation.21 | loop fusion | bytes 8388612 | tf_op jit(solution)/shard_map/while/body/eval_jaxpr/cond/branch_1_fun/dynamic_slice | solution.py:159
  183.1 8.1 %fusion.18 = f32[4,512,8,256]{3,1,2,0:T(8,128)} fusion(bf16[512,4,8,128]{0,3,2,1:T(8,128)(2,1)S(1)} %bitcast.220, bf16[256,4,128]{2,0,1:T(8,128)(2,1)S(1)} %get-tuple-element.449), kind=kOutput, calls=%fused_computation.16 | convolution fusion | flops 1073741824 | bytes 21233664 | tf_op jit(solution)/shard_map/while/body/eval_jaxpr/cond/branch_1_fun/ihgd,jhd->hgij/dot_general | solution.py:169
  191.2 11.8 %fusion.15 = f32[4,128,256,1]{2,1,3,0:T(8,128)S(1)} fusion(bf16[512,4,8,128]{0,3,2,1:T(8,128)(2,1)} %bitcast.221, f32[4,512,8,256]{3,1,2,0:T(8,128)} %fusion.18, bf16[512,4,8,128]{0,3,2,1:T(8,128)(2,1)} %bitcast.222, f32[4,8,512]{2,1,0:T(8,128)S(1)} %dynamic-slice_bitcast_fusion, f32[4,8,512]{2,1,0:T(8,128)S(1)} %dynamic-slice_bitcast_fusion.1, ...), kind=kOutput, calls=%fused_computation.12 | convolution fusion | flops 2172649472 | bytes 26214400 | tf_op jit(solution)/shard_map/while/body/eval_jaxpr/cond/branch_1_fun/hgij,ihgd->jhd/dot_general | solution.py:181
  203.0 9.1 %fusion.12 = f32[4,128,256,1]{2,1,3,0:T(8,128)S(1)} fusion(bf16[512,4,8,128]{0,3,2,1:T(8,128)(2,1)} %bitcast.223, f32[4,512,8,256]{3,1,2,0:T(8,128)} %fusion.18, f32[4,8,512]{2,1,0:T(8,128)S(1)} %dynamic-slice_bitcast_fusion.1, pred[512,256]{1,0:T(8,128)(4,1)S(1)} %broadcast_compare_fusion), kind=kOutput, calls=%fused_computation.10 | convolution fusion | flops 1090519040 | bytes 21692416 | tf_op jit(solution)/shard_map/while/body/eval_jaxpr/cond/branch_1_fun/hgij,ihgd->jhd/dot_general | solution.py:184
  213.6 37.1 %conditional.4 = ((f32[256,512]{0,1:T(8,128)S(1)}, f32[256,512]{0,1:T(8,128)S(1)})) conditional(s32[]{:T(128)} %convert_element_type.67, (f32[256,512]{0,1:T(8,128)S(1)}, f32[256,512]{0,1:T(8,128)S(1)}) %tuple.139, (s32[]{:T(128)}, bf16[1024,4096]{0,1:T(8,128)(2,1)}, s32[]{:T(128)}, s32[512]{0:T(512)S(1)}, bf16[256,4,128]{2,0,1:T(8,128)(2,1)S(1)}, ...), branch_computations={%region_12.12_spmd, %region_13.13_spmd} | conditional | flops 4337303552 | bytes 139793536 | solution.py:192
  213.8 2.6 constant_dynamic-slice_fusion.1
  218.3 2.9 %constant_dynamic-slice_fusion = bf16[512,4096]{0,1:T(8,128)(2,1)} fusion(bf16[1024,4096]{0,1:T(8,128)(2,1)S(1)} %copy-done.1, s32[]{:T(128)S(6)} %select_n.81), kind=kLoop, calls=%fused_computation.21 | loop fusion | bytes 8388612 | tf_op jit(solution)/shard_map/while/body/eval_jaxpr/cond/branch_1_fun/dynamic_slice | solution.py:159
  221.5 8.1 %fusion.18 = f32[4,512,8,256]{3,1,2,0:T(8,128)} fusion(bf16[512,4,8,128]{0,3,2,1:T(8,128)(2,1)S(1)} %bitcast.220, bf16[256,4,128]{2,0,1:T(8,128)(2,1)S(1)} %get-tuple-element.449), kind=kOutput, calls=%fused_computation.16 | convolution fusion | flops 1073741824 | bytes 21233664 | tf_op jit(solution)/shard_map/while/body/eval_jaxpr/cond/branch_1_fun/ihgd,jhd->hgij/dot_general | solution.py:169
  229.6 11.8 %fusion.15 = f32[4,128,256,1]{2,1,3,0:T(8,128)S(1)} fusion(bf16[512,4,8,128]{0,3,2,1:T(8,128)(2,1)} %bitcast.221, f32[4,512,8,256]{3,1,2,0:T(8,128)} %fusion.18, bf16[512,4,8,128]{0,3,2,1:T(8,128)(2,1)} %bitcast.222, f32[4,8,512]{2,1,0:T(8,128)S(1)} %dynamic-slice_bitcast_fusion, f32[4,8,512]{2,1,0:T(8,128)S(1)} %dynamic-slice_bitcast_fusion.1, ...), kind=kOutput, calls=%fused_computation.12 | convolution fusion | flops 2172649472 | bytes 26214400 | tf_op jit(solution)/shard_map/while/body/eval_jaxpr/cond/branch_1_fun/hgij,ihgd->jhd/dot_general | solution.py:181
  241.4 9.1 %fusion.12 = f32[4,128,256,1]{2,1,3,0:T(8,128)S(1)} fusion(bf16[512,4,8,128]{0,3,2,1:T(8,128)(2,1)} %bitcast.223, f32[4,512,8,256]{3,1,2,0:T(8,128)} %fusion.18, f32[4,8,512]{2,1,0:T(8,128)S(1)} %dynamic-slice_bitcast_fusion.1, pred[512,256]{1,0:T(8,128)(4,1)S(1)} %broadcast_compare_fusion), kind=kOutput, calls=%fused_computation.10 | convolution fusion | flops 1090519040 | bytes 21692416 | tf_op jit(solution)/shard_map/while/body/eval_jaxpr/cond/branch_1_fun/hgij,ihgd->jhd/dot_general | solution.py:184
  256.9 3.6 %collective-permute-done.1 = bf16[2,128,512]{2,1,0:T(8,128)(2,1)S(1)} collective-permute-done((bf16[2,128,512]{2,1,0:T(8,128)(2,1)}, bf16[2,128,512]{2,1,0:T(8,128)(2,1)S(1)}, u32[]{:S(2)}, u32[]{:S(2)}) %collective-permute-start.1) | collective-permute-done | bytes 262176 | tf_op jit(solution)/shard_map/ppermute | solution.py:14
  (83 shorter events, 37.3 us)
Async XLA Ops:
  7.2 50.5 %all-gather.6.cloned.1.call-start = ((), (), s32[]{:S(2)}) async-start(), calls=%async_computation | async-start | bytes 4718592 | tf_op jit(solution)/shard_map/all_gather | solution.py:119
  9.0 9.4 %collective-permute-start = (bf16[2,128,512]{2,1,0:T(8,128)(2,1)S(1)}, bf16[2,128,512]{2,1,0:T(8,128)(2,1)S(1)}, u32[]{:S(2)}, u32[]{:S(2)}) collective-permute-start(bf16[2,128,512]{2,1,0:T(8,128)(2,1)S(1)} %constant_dynamic-update-slice_fusion), channel_id=1, source_target_pairs={{0,1},{1,0},{2,3},{3,2},{4,5},{5,4},{6,7},{7,6},{8,9},{9,8},{10,11... | collective-permute-start | bytes 786440 | tf_op jit(solution)/shard_map/ppermute | solution.py:14
  19.5 10.1 %copy-start.3 = (bf16[2,256,512]{2,1,0:T(8,128)(2,1)S(1)}, bf16[2,256,512]{2,1,0:T(8,128)(2,1)}, u32[]{:S(2)}) copy-start(bf16[2,256,512]{2,1,0:T(8,128)(2,1)} %maximum_select_fusion) | copy-start | bytes 1572868
  19.5 141.5 %all-gather.8.cloned.1.call-start = ((), (), s32[]{:S(2)}) async-start(), calls=%async_computation.1 | async-start | bytes 9437184 | tf_op jit(solution)/shard_map/all_gather | solution.py:140
  21.9 151.8 %all-gather.10.cloned.1.call-start = ((), (), s32[]{:S(2)}) async-start(), calls=%async_computation.2 | async-start | bytes 9437184 | tf_op jit(solution)/shard_map/all_gather | solution.py:141
  74.0 12.6 %copy-start.2 = (bf16[1,128,4096]{1,2,0:T(8,128)(2,1)S(1)}, bf16[1,128,4096]{1,2,0:T(8,128)(2,1)}, u32[]{:S(2)}) copy-start(bf16[1,128,4096]{1,2,0:T(8,128)(2,1)} %copy.74) | copy-start | bytes 3145732
  146.3 27.5 %copy-start.4 = (bf16[256,4,128]{2,0,1:T(8,128)(2,1)S(1)}, bf16[256,4,128]{2,0,1:T(8,128)(2,1)}, u32[]{:S(2)}) copy-start(bf16[256,4,128]{2,0,1:T(8,128)(2,1)} %copy.87) | copy-start | bytes 786436
  175.2 4.6 %copy-start.1 = (bf16[1024,4096]{0,1:T(8,128)(2,1)S(1)}, bf16[1024,4096]{0,1:T(8,128)(2,1)}, u32[]{:S(2)}) copy-start(bf16[1024,4096]{0,1:T(8,128)(2,1)} %get-tuple-element.451) | copy-start | bytes 25165828 | tf_op jit(solution)/shard_map/while/body/eval_jaxpr/cond
  179.8 3.2 %copy-start = (bf16[512,4096]{0,1:T(8,128)(2,1)}, bf16[512,4096]{0,1:T(8,128)(2,1)S(1)}, u32[]{:S(2)}) copy-start(bf16[512,4096]{0,1:T(8,128)(2,1)S(1)} %constant_dynamic-slice_fusion.1) | copy-start | bytes 12582916 | tf_op jit(solution)/shard_map/while/body/eval_jaxpr/cond
  213.6 4.6 %copy-start.1 = (bf16[1024,4096]{0,1:T(8,128)(2,1)S(1)}, bf16[1024,4096]{0,1:T(8,128)(2,1)}, u32[]{:S(2)}) copy-start(bf16[1024,4096]{0,1:T(8,128)(2,1)} %get-tuple-element.451) | copy-start | bytes 25165828 | tf_op jit(solution)/shard_map/while/body/eval_jaxpr/cond
  218.3 3.2 %copy-start = (bf16[512,4096]{0,1:T(8,128)(2,1)}, bf16[512,4096]{0,1:T(8,128)(2,1)S(1)}, u32[]{:S(2)}) copy-start(bf16[512,4096]{0,1:T(8,128)(2,1)S(1)} %constant_dynamic-slice_fusion.1) | copy-start | bytes 12582916 | tf_op jit(solution)/shard_map/while/body/eval_jaxpr/cond
  251.9 8.7 %collective-permute-start.1 = (bf16[2,128,512]{2,1,0:T(8,128)(2,1)}, bf16[2,128,512]{2,1,0:T(8,128)(2,1)S(1)}, u32[]{:S(2)}, u32[]{:S(2)}) collective-permute-start(bf16[2,128,512]{2,1,0:T(8,128)(2,1)} %pad_maximum_fusion), channel_id=1, source_target_pairs={{0,1},{1,0},{2,3},{3,2},{4,5},{5,4},{6,7},{7,6},{8,9},{9,8},{10,11... | collective-permute-start | bytes 786440 | tf_op jit(solution)/shard_map/ppermute | solution.py:14
Sparse Core Ops, SparseCore 0:
  19.6 37.9 all-gather.5
  59.5 55.8 all-gather.7
  117.3 56.3 all-gather.9
where the time goes:
time: 269 us; the launch traced here: 268 us
  matrix products  78.8 us (29%)
  blocking collectives  56 us (21%)
  local copies, waits for them, and re-layouts  51.5 us (19%)
  waiting for transfers between devices  49.7 us (18%)
  between operations  14.6 us (5%)
  other arithmetic  11.2 us (4%)
  starting transfers between devices  4.72 us (2%)
    all_gather x1, blocking collectives, on_device(): lax.all_gather(total_rows, 'ctx', axis=0, tiled=True)  45.8 us
    all_gather x1, waiting for transfers between devices, on_device(): gathered_pairs = lax.all_gather(block_pairs, 'ctx', axis=1, tiled=True)  26.9 us
    dot_general x2, matrix products, accumulate(): jnp.einsum('hgij,ihgd->jhd', score_grad, query_block, preferred_element_t...  23.6 us
    unnamed x18, local copies, waits for them, and re-layouts  19.3 us
    dot_general x2, matrix products, accumulate(): jnp.einsum('hgij,ihgd->jhd', weights, grad_block, preferred_element_type=...  18.1 us
    dot_general x2, matrix products, accumulate(): jnp.einsum('ihgd,jhd->hgij', query_block, block_keys, preferred_element_t...  16.3 us
    all_gather x1, waiting for transfers between devices, on_device(): grad_piece = lax.all_gather(grad_local, 'ctx', axis=0, tiled=True)  12.8 us
    all_gather x1, blocking collectives, on_device(): lax.all_gather(dot_rows, 'ctx', axis=0, tiled=True)  10.2 us
  transfers between devices with their start and end apart: 5, of which 4 were waited for; matrix products, arithmetic and copies ran while one was open for 23% of the time, Pallas kernels for 0%

commit v1 on v0

v1 whole, which is shorter than its diff:
```python
import functools
import math

import jax
import jax.numpy as jnp
from jax import lax
from jax.experimental import pallas as pl
from jax.experimental.pallas import tpu as pltpu
from jax.sharding import PartitionSpec as P

HD = 128
NT = (((1,), (1,)), ((), ()))
TN = (((0,), (0,)), ((), ()))
F32 = jnp.float32
BF16 = jnp.bfloat16


def dot(a, b, dims=(((1,), (0,)), ((), ()))):
    return lax.dot_general(a, b, dims, preferred_element_type=F32)


def attend_kernel(rows, sharing, q_ref, g_ref, k_ref, v_ref, o_ref, dq_ref, dk_ref, dv_ref,
                  s_scr, p_scr, qs, gs, qn, gn, acc, top, total, drow):
    block = lax.axis_index("ctx")
    half = lax.axis_index("head") % 2
    span = 2 * rows
    wide = rows * sharing
    step_cols = 2 * rows
    scaling = 1.0 / math.sqrt(HD)
    factor = scaling * math.log2(math.e)
    for h in range(sharing):
        qs[h * rows:(h + 1) * rows, :] = q_ref[:, h * HD:(h + 1) * HD]
        gs[h * rows:(h + 1) * rows, :] = g_ref[:, h * HD:(h + 1) * HD]
    dk_ref[...] = jnp.zeros_like(dk_ref)
    dv_ref[...] = jnp.zeros_like(dv_ref)

    def keys_at(b):
        return pl.ds(pl.multiple_of(b * span, span), span)

    top[...] = jnp.full_like(top, -jnp.inf)

    def scores(b, masked):
        kb = k_ref[keys_at(b), :]
        for c in range(0, wide, step_cols):
            cols = slice(c, c + step_cols)
            s = dot(kb, qs[cols, :], NT)
            if masked:
                key_pos = lax.broadcasted_iota(jnp.int32, s.shape, 0)
                row_pos = half * rows + lax.broadcasted_iota(jnp.int32, s.shape, 1) % rows
                s = jnp.where(key_pos <= row_pos, s, -jnp.inf)
            s_scr[keys_at(b), cols] = s
            top[:, cols] = jnp.maximum(top[:, cols], s.reshape(span // 8, 8, step_cols).max(axis=0))

    @pl.loop(0, block)
    def _(b):
        scores(b, False)

    scores(block, True)
    highest = jnp.max(top[...], axis=0, keepdims=True) * factor
    total[...] = jnp.zeros_like(total)
    acc[...] = jnp.zeros_like(acc)

    @pl.loop(0, block + 1)
    def _(b):
        vb = v_ref[keys_at(b), :]
        for c in range(0, wide, step_cols):
            cols = slice(c, c + step_cols)
            p = jnp.exp2(s_scr[keys_at(b), cols] * factor - highest[:, cols])
            total[:, cols] += p.reshape(span // 8, 8, step_cols).sum(axis=0)
            pb = p.astype(BF16)
            p_scr[keys_at(b), cols] = pb
            acc[cols, :] += dot(pb, vb, TN)

    inverse = 1.0 / jnp.sum(total[...], axis=0, keepdims=True)
    turned = []
    for h in range(sharing):
        part = slice(h * rows, (h + 1) * rows)
        inv = jnp.broadcast_to(inverse[:, part], (HD, rows)).T
        turned.append(inv)
        out = (acc[part, :] * inv).astype(BF16)
        o_ref[:, h * HD:(h + 1) * HD] = out
        g = gs[part, :].astype(F32)
        drow[:, part] = jnp.sum((g * out.astype(F32)).T, axis=0, keepdims=True)
        gn[part, :] = (g * inv).astype(BF16)
        qn[part, :] = (qs[part, :].astype(F32) * (inv * scaling)).astype(BF16)
    acc[...] = jnp.zeros_like(acc)

    @pl.loop(0, block + 1)
    def _(b):
        kb = k_ref[keys_at(b), :]
        vb = v_ref[keys_at(b), :]
        dk = jnp.zeros((span, HD), F32)
        dv = jnp.zeros((span, HD), F32)
        for c in range(0, wide, step_cols):
            cols = slice(c, c + step_cols)
            dp = dot(vb, gs[cols, :], NT)
            pb = p_scr[keys_at(b), cols]
            ds = (pb.astype(F32) * (dp - drow[:, cols])).astype(BF16)
            dk += dot(ds, qn[cols, :])
            dv += dot(pb, gn[cols, :])
            acc[cols, :] += dot(ds, kb, TN)
        dk_ref[keys_at(b), :] = dk.astype(dk_ref.dtype)
        dv_ref[keys_at(b), :] = dv.astype(dv_ref.dtype)

    for h in range(sharing):
        part = slice(h * rows, (h + 1) * rows)
        inv = jnp.broadcast_to(inverse[:, part], (HD, rows)).T
        dq_ref[:, h * HD:(h + 1) * HD] = acc[part, :] * (inv * scaling)


def attend(q, g, k_all, v_all):
    rows, width = q.shape
    seq, pair_width = k_all.shape
    pairs = pair_width // HD
    sharing = width // pair_width
    wide = rows * sharing
    by_head = lambda r, w: pl.BlockSpec((r, w), lambda i: (0, i))
    return pl.pallas_call(
        functools.partial(attend_kernel, rows, sharing),
        grid=(pairs,),
        out_shape=(
            jax.ShapeDtypeStruct((rows, width), BF16),
            jax.ShapeDtypeStruct((rows, width), F32),
            jax.ShapeDtypeStruct((seq, pair_width), F32),
            jax.ShapeDtypeStruct((seq, pair_width), F32),
        ),
        in_specs=[by_head(rows, sharing * HD)] * 2 + [by_head(seq, HD)] * 2,
        out_specs=(by_head(rows, sharing * HD), by_head(rows, sharing * HD), by_head(seq, HD), by_head(seq, HD)),
        scratch_shapes=[
            pltpu.VMEM((seq, wide), F32),
            pltpu.VMEM((seq, wide), BF16),
            pltpu.VMEM((wide, HD), BF16),
            pltpu.VMEM((wide, HD), BF16),
            pltpu.VMEM((wide, HD), BF16),
            pltpu.VMEM((wide, HD), BF16),
            pltpu.VMEM((wide, HD), F32),
            pltpu.VMEM((8, wide), F32),
            pltpu.VMEM((8, wide), F32),
            pltpu.VMEM((1, wide), F32),
        ],
        compiler_params=pltpu.CompilerParams(vmem_limit_bytes=60 * 1024 * 1024),
        name="attend",
    )(q, g, k_all, v_all)


def from_partner(value):
    pairs = [(source, source ^ 1) for source in range(lax.axis_size("head"))]
    return lax.ppermute(value, "head", pairs)


def on_device(query_input, key_input, value_input, grad_input):
    rows = query_input.shape[1]
    pair_width = key_input.shape[2]
    blocks = lax.axis_size("ctx")
    half = lax.axis_index("head") % 2
    own = jnp.concatenate([key_input[0], value_input[0]], axis=1)
    other = from_partner(own)
    both = jnp.where(half == 0, jnp.concatenate([own, other], axis=0), jnp.concatenate([other, own], axis=0))
    gathered = lax.all_gather(both, "ctx", axis=0, tiled=True)
    attended, query_grad, dk, dv = attend(
        query_input[0], grad_input[0], gathered[:, :pair_width], gathered[:, pair_width:]
    )
    sums = jnp.concatenate([dk, dv], axis=1)
    sums = lax.psum_scatter(sums, "ctx", scatter_dimension=0, tiled=True)
    outgoing = lax.dynamic_slice_in_dim(sums, (1 - half) * rows, rows, 0).astype(BF16)
    mine = lax.dynamic_slice_in_dim(sums, half * rows, rows, 0) + from_partner(outgoing).astype(F32)
    return (attended[None], query_grad[None], mine[None, :, :pair_width], mine[None, :, pair_width:])


def solution(mesh):
    spec = P("ctx", "head", None)
    return jax.shard_map(on_device, mesh=mesh, in_specs=(spec,) * 4, out_specs=(spec,) * 4, check_vma=False)
```

time: 269 us -> 225 us (0.84)
  waiting for transfers between devices: 49.7 us -> 173 us
  matrix products: 78.8 us -> 0 us
  blocking collectives: 56 us -> 0 us
  local copies, waits for them, and re-layouts: 51.5 us -> 6.37 us
  Pallas kernels: 0 us -> 13.5 us
    reduce_scatter x0 -> x1, waiting for transfers between devices: none -> 122 us  [on_device(): sums = lax.psum_scatter(sums, 'ctx', scatter_dimension=0, tiled=True)]
    dot_general x10 -> x0, matrix products: 78.8 us -> none  [the longest x2 23.6 us: accumulate(): jnp.einsum('hgij,ihgd->jhd', score_grad, query_block, preferred_element_t...]
    all_gather x2 -> x0, blocking collectives: 56 us -> none  [the longest x1 45.8 us: on_device(): lax.all_gather(total_rows, 'ctx', axis=0, tiled=True)]
    unnamed x18 -> x0, local copies, waits for them, and re-layouts: 19.3 us -> none
    dynamic_slice x7 -> x0, local copies, waits for them, and re-layouts: 14.9 us -> none  [the longest x2 5.8 us: accumulate(): lax.dynamic_slice_in_dim(grad_piece, offset, query_span, 0)]
    pallas_call x0 -> x1, Pallas kernels: none -> 13.5 us  [attend(): pl.pallas_call(functools.partial(attend_kernel, rows, sharing), grid=(pai...]
    concatenate x0 -> x2, other arithmetic: none -> 9.15 us  [the longest x1 8.16 us: on_device(): sums = jnp.concatenate([dk, dv], axis=1)]
    slice x2 -> x1, local copies, waits for them, and re-layouts: 0.17 us -> 4.47 us  [on_device(): gathered[:, pair_width:]]
  transfers between devices with their start and end apart: 5 -> 4, of which waited for: 4 -> 4; matrix products, arithmetic and copies ran while one was open for 23% -> 0% of each run, Pallas kernels for 0% -> 0%
where the time goes in v1:
time: 225 us; the launch traced here: 224 us
  waiting for transfers between devices  173 us (77%)
  between operations  14.1 us (6%)
  Pallas kernels  13.5 us (6%)
  other arithmetic  12.3 us (5%)
  local copies, waits for them, and re-layouts  6.37 us (3%)
  starting transfers between devices  4.75 us (2%)
    reduce_scatter x1, waiting for transfers between devices, on_device(): sums = lax.psum_scatter(sums, 'ctx', scatter_dimension=0, tiled=True)  122 us
    all_gather x1, waiting for transfers between devices, on_device(): gathered = lax.all_gather(both, 'ctx', axis=0, tiled=True)  38.1 us
    pallas_call x1, Pallas kernels, attend(): pl.pallas_call(functools.partial(attend_kernel, rows, sharing), grid=(pai...  13.5 us
    ppermute x2, waiting for transfers between devices, from_partner(): return lax.ppermute(value, 'head', pairs)  12.7 us
    concatenate x1, other arithmetic, on_device(): sums = jnp.concatenate([dk, dv], axis=1)  8.16 us
    ppermute x2, starting transfers between devices, from_partner(): return lax.ppermute(value, 'head', pairs)  4.67 us
  transfers between devices with their start and end apart: 4, of which 4 were waited for; matrix products, arithmetic and copies ran while one was open for 0% of the time, Pallas kernels for 0%

profile of v1, /device:TPU:0, one launch (start us, length us, event | category | flops | bytes accessed | tf_op | source)
XLA Modules:
  0.0 224.3 jit_solution(18379584927555700270)
XLA Ops:
  7.2 0.0 all-gather.2.cloned.1.call-start
  7.2 1.0 pad_maximum_fusion.1
  8.2 3.1 %collective-permute-start = (bf16[128,1024]{1,0:T(8,128)(2,1)S(1)}, bf16[128,1024]{1,0:T(8,128)(2,1)S(1)}, u32[]{:S(2)}, u32[]{:S(2)}) collective-permute-start(bf16[128,1024]{1,0:T(8,128)(2,1)S(1)} %pad_maximum_fusion.1), channel_id=1, source_target_pairs={{0,1},{1,0},{2,3},{3,2},{4,5},{5,4},{6,7},{7,6},{8,9},{9,8},{10,11... | collective-permute-start | bytes 786440 | tf_op jit(solution)/shard_map/ppermute | solution.py:148
  11.3 6.3 %collective-permute-done = bf16[128,1024]{1,0:T(8,128)(2,1)S(1)} collective-permute-done((bf16[128,1024]{1,0:T(8,128)(2,1)S(1)}, bf16[128,1024]{1,0:T(8,128)(2,1)S(1)}, u32[]{:S(2)}, u32[]{:S(2)}) %collective-permute-start) | collective-permute-done | bytes 262176 | tf_op jit(solution)/shard_map/ppermute | solution.py:148
  17.6 2.1 maximum_select_fusion
  19.7 0.0 all-gather.2.cloned.1.call-update
  19.7 0.0 reduce-scatter.2.cloned.1.call-start
  19.8 38.1 %all-gather.2.cloned.1.call-done = bf16[2048,1024]{1,0:T(8,128)(2,1)} async-done(((bf16[256,1024]{1,0:T(8,128)(2,1)}), bf16[2048,1024]{1,0:T(8,128)(2,1)}) %all-gather.2.cloned.1.call-update) | async-done | bytes 4194320 | tf_op jit(solution)/shard_map/all_gather | solution.py:159
  57.9 4.5 %fusion = (bf16[2048,512]{1,0:T(8,128)(2,1)}, bf16[2048,512]{1,0:T(8,128)(2,1)}) fusion(bf16[2048,1024]{1,0:T(8,128)(2,1)} %all-gather.2.cloned.1.call-done), kind=kLoop, calls=%fused_computation.7 | loop fusion | bytes 8388608 | tf_op jit(solution)/shard_map/slice | solution.py:161
  62.3 13.5 %attend.1 = (bf16[128,4096]{1,0:T(8,128)(2,1)}, f32[128,4096]{1,0:T(8,128)}, f32[2048,512]{1,0:T(8,128)}, f32[2048,512]{1,0:T(8,128)}) custom-call(bf16[128,4096]{1,0:T(8,128)(2,1)} %bitcast.10, bf16[128,4096]{1,0:T(8,128)(2,1)} %bitcast.11, bf16[2048,512]{1,0:T(8,128)(2,1)} %get-tuple-element.13.k_ref, bf16[2048,512]{1,0:T(8,128)(2,1)} %get-tuple-element.12.v_ref), custom_call_target="tpu_custom_call" | custom-call | tf_op jit(solution)/shard_map/attend/pallas_call | solution.py:118
  75.8 8.2 %pad_maximum_fusion = f32[2048,1024]{1,0:T(8,128)} fusion(f32[2048,512]{1,0:T(8,128)} %get-tuple-element.11, f32[2048,512]{1,0:T(8,128)} %get-tuple-element.10), kind=kLoop, calls=%fused_computation | loop fusion | flops 2097152 | bytes 16777216 | tf_op jit(solution)/shard_map/concatenate | solution.py:163
  84.0 0.0 reduce-scatter.2.cloned.1.call-update
  84.0 122.5 %reduce-scatter.2.cloned.1.call-done = f32[256,1024]{1,0:T(8,128)} async-done(((f32[2048,1024]{1,0:T(8,128)}), f32[256,1024]{1,0:T(8,128)}) %reduce-scatter.2.cloned.1.call-update) | async-done | bytes 1048592 | tf_op jit(solution)/shard_map/reduce_scatter | solution.py:164
  206.5 1.1 dynamic-slice_convert_fusion
  207.5 1.6 collective-permute-start.1
  209.1 6.4 %collective-permute-done.1 = bf16[128,1024]{1,0:T(8,128)(2,1)S(1)} collective-permute-done((bf16[128,1024]{1,0:T(8,128)(2,1)S(1)}, bf16[128,1024]{1,0:T(8,128)(2,1)S(1)}, u32[]{:S(2)}, u32[]{:S(2)}) %collective-permute-start.1) | collective-permute-done | bytes 262176 | tf_op jit(solution)/shard_map/ppermute | solution.py:148
  215.5 1.1 convert_add_fusion
  216.6 0.8 slice_bitcast_fusion
Async XLA Ops:
  7.2 50.7 %all-gather.2.cloned.1.call-start = ((), (), s32[]{:S(2)}) async-start(), calls=%async_computation.1 | async-start | bytes 4718592 | tf_op jit(solution)/shard_map/all_gather | solution.py:159
  8.2 9.4 %collective-permute-start = (bf16[128,1024]{1,0:T(8,128)(2,1)S(1)}, bf16[128,1024]{1,0:T(8,128)(2,1)S(1)}, u32[]{:S(2)}, u32[]{:S(2)}) collective-permute-start(bf16[128,1024]{1,0:T(8,128)(2,1)S(1)} %pad_maximum_fusion.1), channel_id=1, source_target_pairs={{0,1},{1,0},{2,3},{3,2},{4,5},{5,4},{6,7},{7,6},{8,9},{9,8},{10,11... | collective-permute-start | bytes 786440 | tf_op jit(solution)/shard_map/ppermute | solution.py:148
  19.7 186.8 %reduce-scatter.2.cloned.1.call-start = ((), (), s32[]{:S(2)}) async-start(), calls=%async_computation.2 | async-start | bytes 9437184 | tf_op jit(solution)/shard_map/reduce_scatter | solution.py:164
  207.5 7.9 %collective-permute-start.1 = (bf16[128,1024]{1,0:T(8,128)(2,1)S(1)}, bf16[128,1024]{1,0:T(8,128)(2,1)S(1)}, u32[]{:S(2)}, u32[]{:S(2)}) collective-permute-start(bf16[128,1024]{1,0:T(8,128)(2,1)S(1)} %dynamic-slice_convert_fusion), channel_id=1, source_target_pairs={{0,1},{1,0},{2,3},{3,2},{4,5},{5,4},{6,7},{7,6},{8,9},{9,8},{10,11... | collective-permute-start | bytes 786440 | tf_op jit(solution)/shard_map/ppermute | solution.py:148
Sparse Core Ops, SparseCore 0:
  19.8 37.9 all-gather.1
  84.1 122.3 reduce-scatter.1

commit v2 on v1

v2 whole, which is shorter than its diff:
```python
import functools
import math

import jax
import jax.numpy as jnp
from jax import lax
from jax.experimental import pallas as pl
from jax.experimental.pallas import tpu as pltpu
from jax.sharding import PartitionSpec as P

HD = 128
NT = (((1,), (1,)), ((), ()))
TN = (((0,), (0,)), ((), ()))
F32 = jnp.float32
BF16 = jnp.bfloat16


def dot(a, b, dims=(((1,), (0,)), ((), ()))):
    return lax.dot_general(a, b, dims, preferred_element_type=F32)


MESH = pl.DeviceIdType.MESH


def pieces_of(rows):
    unit = 16
    units = rows // unit
    count = min(3, units)
    sizes = [(units // count + (1 if i < units % count else 0)) * unit for i in range(count)]
    starts = [sum(sizes[:i]) for i in range(count)]
    return [slice(a, a + s) for a, s in zip(starts, sizes)]


def orders_of(bits, count):
    links = [d for d in range(bits + 1) if d != bits - 1]
    return [[links[(i + p) % len(links)] for i in range(len(links))] for p in range(count)]


def my_bits(bits):
    block = lax.axis_index("ctx")
    return [block // 2 ** (bits - 1 - d) % 2 for d in range(bits)] + [lax.axis_index("head") % 2]


def partner_of(bits, me, d):
    if d == bits:
        return {"head": lax.axis_index("head") + 1 - 2 * me[d]}
    return {"ctx": lax.axis_index("ctx") + (1 - 2 * me[d]) * 2 ** (bits - 1 - d)}


def mirror_of(bits):
    return {"ctx": 2 ** bits - 1 - lax.axis_index("ctx")}


def greet(bits, me):
    barrier = pltpu.get_barrier_semaphore()
    for d in range(bits + 1):
        pl.semaphore_signal(barrier, inc=1, device_id=partner_of(bits, me, d), device_id_type=MESH)
    pl.semaphore_signal(barrier, inc=1, device_id=mirror_of(bits), device_id_type=MESH)
    pl.semaphore_wait(barrier, bits + 2)


def gather_steps(bits, me, arrays, heads, parts, sems):
    link_send, link_recv, core_send, core_recv = sems
    orders = orders_of(bits, len(parts))
    regions = [list(me) for _ in parts]
    fresh = [list(me) for _ in parts]
    links, cores = [], []

    def copy(ref, index, d, send, recv):
        return pltpu.make_async_remote_copy(
            src_ref=ref.at[index], dst_ref=ref.at[index], send_sem=send, recv_sem=recv,
            device_id=partner_of(bits, me, d), device_id_type=MESH)

    def step(k):
        for c in links:
            c.wait()
        links.clear()
        for p in range(len(parts)):
            if 0 < k <= bits:
                d = orders[p][k - 1]
                fresh[p] = list(regions[p])
                fresh[p][d] = 1 - me[d]
                regions[p][d] = slice(None)
        for p, part in enumerate(parts):
            for a, ref in enumerate(arrays):
                if k < bits:
                    c = copy(ref, (heads, *regions[p], part), orders[p][k], link_send.at[p, k, a], link_recv.at[p, k, a])
                    c.start()
                    links.append(c)
        for p, part in enumerate(parts):
            for a, ref in enumerate(arrays):
                if k <= bits:
                    c = copy(ref, (heads, *fresh[p], part), bits - 1, core_send.at[p, k, a], core_recv.at[p, k, a])
                    c.start()
                    cores.append(c)
        if k > bits:
            for c in cores:
                c.wait()

    return [functools.partial(step, k) for k in range(bits + 2)]


def scatter_steps(bits, me, arrays, outs, h, parts, held, send_sem, recv_sem):
    orders = [[bits - 1] + order[::-1] for order in orders_of(bits, len(parts))]
    now = [[(ref, (part,)) for ref in arrays] for part in parts]
    dims = [list(range(bits + 1)) for _ in parts]
    copies = []

    def pick(p, d, value, tail):
        return (h, *(value if e == d else slice(None) for e in dims[p]), *tail)

    def step(k):
        if k > 0:
            for p, part in enumerate(parts):
                d = orders[p][k - 1]
                for a in range(2):
                    copies[2 * p + a].wait()
                    ref, tail = now[p][a]
                    slot = held[p][k - 1][a]
                    sums = ref[pick(p, d, me[d], tail)].astype(F32) + slot[h].astype(F32)
                    if k > bits:
                        outs[a][part, h * HD:(h + 1) * HD] = sums
                    else:
                        slot[h] = sums.astype(slot.dtype)
                    now[p][a] = (slot, (slice(None),))
                dims[p].remove(d)
            copies.clear()
        if k <= bits:
            for p in range(len(parts)):
                d = orders[p][k]
                for a in range(2):
                    ref, tail = now[p][a]
                    c = pltpu.make_async_remote_copy(
                        src_ref=ref.at[pick(p, d, 1 - me[d], tail)], dst_ref=held[p][k][a].at[h],
                        send_sem=send_sem.at[p, k, a], recv_sem=recv_sem.at[p, k, a],
                        device_id=partner_of(bits, me, d), device_id_type=MESH)
                    c.start()
                    copies.append(c)

    return [functools.partial(step, k) for k in range(bits + 2)]


def layer_kernel(bits, sharing, q_ref, g_ref, k_ref, v_ref, o_ref, dq_ref, ok_ref, ov_ref,
                 ka, va, dka, dva, s_scr, p_scr, qs, gs, qn, gn, acc, top, total, drow,
                 qm, gm, om, dm, oin, din, swap_send, swap_recv,
                 own_sem, link_send, link_recv, core_send, core_recv, send_sem, recv_sem, *slots):
    rows, pair_width = k_ref.shape
    pairs = pair_width // HD
    block = lax.axis_index("ctx")
    half = lax.axis_index("head") % 2
    span = 2 * rows
    wide = rows * sharing
    step_cols = 2 * rows
    scaling = 1.0 / math.sqrt(HD)
    factor = scaling * math.log2(math.e)
    me = my_bits(bits)
    parts = pieces_of(rows)
    slot_list = iter(slots)
    held = [[[next(slot_list) for _ in range(2)] for _ in range(bits + 1)] for _ in parts]

    greet(bits, me)
    own = [pltpu.make_async_copy(src.at[:, h * HD:(h + 1) * HD], dst.at[(h, *me)], own_sem.at[h, a])
           for h in range(pairs) for a, (src, dst) in enumerate(((k_ref, ka), (v_ref, va)))]
    for c in own:
        c.start()
    for c in own:
        c.wait()
    groups = [slice(0, 1)] + ([slice(1, pairs)] if pairs > 1 else [])
    gathers = [gather_steps(bits, me, (ka, va), heads, parts,
                            [r.at[i] for r in (link_send, link_recv, core_send, core_recv)])
               for i, heads in enumerate(groups)]
    pending = []

    def advance(count=1):
        for work in pending:
            for _ in range(count):
                if work:
                    work.pop(0)()
        pending[:] = [work for work in pending if work]

    def drain(work):
        while work:
            work.pop(0)()

    def keys_at(b):
        return pl.ds(pl.multiple_of(b * span, span), span)

    def bits_of(b):
        return tuple(b // 2 ** (bits - 1 - d) % 2 for d in range(bits))

    def first_gather_ready():
        drain(gathers[0])
        if len(gathers) > 1:
            gathers[1].pop(0)()

    count = 2 ** bits
    light = block < count // 2
    last = pairs - 1
    last_base = last * sharing * HD
    last_cols = slice(last_base, last_base + sharing * HD)

    def swap(i, src, dst):
        return pltpu.make_async_remote_copy(
            src_ref=src, dst_ref=dst, send_sem=swap_send.at[i], recv_sem=swap_recv.at[i],
            device_id=mirror_of(bits), device_id_type=MESH)

    lend = [swap(0, q_ref.at[:, last_cols], qm), swap(1, g_ref.at[:, last_cols], gm)]
    give = [swap(2, om, oin), swap(3, dm, din)]

    def clear(g, first):
        for ref in (dka, dva):
            @pl.loop(first, count)
            def _(b):
                ref[(g, *bits_of(b))] = jnp.zeros((2, rows, HD), ref.dtype)

    def attend_head(g, q_src, g_src, base, block, out_ref, out_base, dq_out, again, polled):
        for h in range(sharing):
            qs[h * rows:(h + 1) * rows, :] = q_src[:, base + h * HD:base + (h + 1) * HD]
            gs[h * rows:(h + 1) * rows, :] = g_src[:, base + h * HD:base + (h + 1) * HD]

        if not again:
            clear(g, block + 1)
        top[...] = jnp.full_like(top, -jnp.inf)
        if g == 0:
            first_gather_ready()
        if g == 1:
            drain(gathers[1])

        def load(ref, b):
            return ref[(g, *bits_of(b))].reshape(span, HD)

        def scores(b, masked):
            kb = load(ka, b)
            for c in range(0, wide, step_cols):
                cols = slice(c, c + step_cols)
                s = dot(kb, qs[cols, :], NT)
                if masked:
                    key_pos = lax.broadcasted_iota(jnp.int32, s.shape, 0)
                    row_pos = half * rows + lax.broadcasted_iota(jnp.int32, s.shape, 1) % rows
                    s = jnp.where(key_pos <= row_pos, s, -jnp.inf)
                s_scr[keys_at(b), cols] = s
                top[:, cols] = jnp.maximum(top[:, cols], s.reshape(span // 8, 8, step_cols).max(axis=0))

        @pl.loop(0, block)
        def _(b):
            scores(b, False)

        scores(block, True)
        polled()
        highest = jnp.max(top[...], axis=0, keepdims=True) * factor
        total[...] = jnp.zeros_like(total)
        acc[...] = jnp.zeros_like(acc)

        @pl.loop(0, block + 1)
        def _(b):
            vb = load(va, b)
            for c in range(0, wide, step_cols):
                cols = slice(c, c + step_cols)
                p = jnp.exp2(s_scr[keys_at(b), cols] * factor - highest[:, cols])
                total[:, cols] += p.reshape(span // 8, 8, step_cols).sum(axis=0)
                pb = p.astype(BF16)
                p_scr[keys_at(b), cols] = pb
                acc[cols, :] += dot(pb, vb, TN)

        polled()
        inverse = 1.0 / jnp.sum(total[...], axis=0, keepdims=True)
        for h in range(sharing):
            part = slice(h * rows, (h + 1) * rows)
            inv = jnp.broadcast_to(inverse[:, part], (HD, rows)).T
            out = (acc[part, :] * inv).astype(BF16)
            out_ref[:, out_base + h * HD:out_base + (h + 1) * HD] = out
            grad = gs[part, :].astype(F32)
            drow[:, part] = jnp.sum((grad * out.astype(F32)).T, axis=0, keepdims=True)
            gn[part, :] = (grad * inv).astype(BF16)
            qn[part, :] = (qs[part, :].astype(F32) * (inv * scaling)).astype(BF16)
        acc[...] = jnp.zeros_like(acc)

        @pl.loop(0, block + 1)
        def _(b):
            kb = load(ka, b)
            vb = load(va, b)
            dk = jnp.zeros((span, HD), F32)
            dv = jnp.zeros((span, HD), F32)
            for c in range(0, wide, step_cols):
                cols = slice(c, c + step_cols)
                dp = dot(vb, gs[cols, :], NT)
                pb = p_scr[keys_at(b), cols]
                ds = (pb.astype(F32) * (dp - drow[:, cols])).astype(BF16)
                dk += dot(ds, qn[cols, :])
                dv += dot(pb, gn[cols, :])
                acc[cols, :] += dot(ds, kb, TN)
            for ref, add in ((dka, dk), (dva, dv)):
                if again:
                    add = add + load(ref, b).astype(F32)
                ref[(g, *bits_of(b))] = add.astype(ref.dtype).reshape(2, rows, HD)

        for h in range(sharing):
            part = slice(h * rows, (h + 1) * rows)
            inv = jnp.broadcast_to(inverse[:, part], (HD, rows)).T
            dq_out[:, out_base + h * HD:out_base + (h + 1) * HD] = (acc[part, :] * (inv * scaling)).astype(dq_out.dtype)

    for g in range(last):
        polls = []

        def polled():
            if g == 0:
                gathers[1].pop(0)()
                if polls:
                    @pl.when(~light)
                    def _():
                        for c in lend:
                            c.start()
                polls.append(1)
            advance()

        base = g * sharing * HD
        attend_head(g, q_ref, g_ref, base, block, o_ref, base, dq_ref, False, polled)
        advance()
        work = scatter_steps(bits, me, (dka, dva), (ok_ref, ov_ref), g, parts, held, send_sem.at[g], recv_sem.at[g])
        work.pop(0)()
        pending.append(work)

    @pl.when(light)
    def _():
        nothing = lambda: None
        attend_head(last, q_ref, g_ref, last_base, block, o_ref, last_base, dq_ref, False, nothing)
        for c in lend:
            c.wait_recv()
        attend_head(last, qm, gm, 0, count - 1 - block, om, 0, dm, True, nothing)
        for c in give:
            c.start()

    @pl.when(~light)
    def _():
        clear(last, 0)

    work = scatter_steps(bits, me, (dka, dva), (ok_ref, ov_ref), last, parts, held, send_sem.at[last], recv_sem.at[last])
    work.pop(0)()
    pending.append(work)
    while pending:
        advance()

    @pl.when(light)
    def _():
        for c in give:
            c.wait_send()

    @pl.when(~light)
    def _():
        for c in lend:
            c.wait_send()
        for c in give:
            c.wait_recv()
        o_ref[:, last_cols] = oin[...]
        dq_ref[:, last_cols] = din[...].astype(F32)


def layer(bits, q, g, k, v):
    rows, width = q.shape
    pair_width = k.shape[1]
    pairs = pair_width // HD
    sharing = width // pair_width
    wide = rows * sharing
    seq = 2 ** (bits + 1) * rows
    parts = pieces_of(rows)
    count = len(parts)
    vmem = pl.BlockSpec(memory_space=pltpu.VMEM)
    whole = pltpu.VMEM((pairs,) + (2,) * (bits + 1) + (rows, HD), BF16)
    sem = pltpu.SemaphoreType.DMA
    slots = [pltpu.VMEM((pairs,) + (2,) * (bits - k) + (part.stop - part.start, HD), BF16)
             for part in parts for k in range(bits + 1) for _ in range(2)]
    return pl.pallas_call(
        functools.partial(layer_kernel, bits, sharing),
        out_shape=(
            jax.ShapeDtypeStruct((rows, width), BF16),
            jax.ShapeDtypeStruct((rows, width), F32),
            jax.ShapeDtypeStruct((rows, pair_width), F32),
            jax.ShapeDtypeStruct((rows, pair_width), F32),
        ),
        in_specs=[vmem] * 4,
        out_specs=(vmem,) * 4,
        scratch_shapes=[
            whole, whole, whole, whole,
            pltpu.VMEM((seq, wide), F32),
            pltpu.VMEM((seq, wide), BF16),
            pltpu.VMEM((wide, HD), BF16),
            pltpu.VMEM((wide, HD), BF16),
            pltpu.VMEM((wide, HD), BF16),
            pltpu.VMEM((wide, HD), BF16),
            pltpu.VMEM((wide, HD), F32),
            pltpu.VMEM((8, wide), F32),
            pltpu.VMEM((8, wide), F32),
            pltpu.VMEM((1, wide), F32),
            *[pltpu.VMEM((rows, sharing * HD), BF16) for _ in range(6)],
            sem((4,)),
            sem((4,)),
            sem((pairs, 2)),
            sem((2, count, bits, 2)),
            sem((2, count, bits, 2)),
            sem((2, count, bits + 1, 2)),
            sem((2, count, bits + 1, 2)),
            sem((pairs, count, bits + 1, 2)),
            sem((pairs, count, bits + 1, 2)),
        ] + slots,
        compiler_params=pltpu.CompilerParams(collective_id=0, has_side_effects=True, vmem_limit_bytes=60 * 2**20),
        name="layer",
    )(q, g, k, v)


def on_device(query_input, key_input, value_input, grad_input):
    bits = (lax.axis_size("ctx") - 1).bit_length()
    outs = layer(bits, query_input[0], grad_input[0], key_input[0], value_input[0])
    return tuple(out[None] for out in outs)


def solution(mesh):
    spec = P("ctx", "head", None)
    return jax.shard_map(on_device, mesh=mesh, in_specs=(spec,) * 4, out_specs=(spec,) * 4, check_vma=False)
```

time: 225 us -> 124 us (0.55)
  waiting for transfers between devices: 173 us -> 0 us
  Pallas kernels: 13.5 us -> 118 us
  between operations: 14.1 us -> 0.65 us
  other arithmetic: 12.3 us -> 0 us
  starting transfers between devices: 4.75 us -> 0 us
    reduce_scatter x1 -> x0, waiting for transfers between devices: 122 us -> none  [on_device(): sums = lax.psum_scatter(sums, 'ctx', scatter_dimension=0, tiled=True)]
    pallas_call x1, Pallas kernels: 13.5 us -> 118 us  [layer(): pl.pallas_call(functools.partial(layer_kernel, bits, sharing), out_shape=...]
    all_gather x1 -> x0, waiting for transfers between devices: 38.1 us -> none  [on_device(): gathered = lax.all_gather(both, 'ctx', axis=0, tiled=True)]
    ppermute x2 -> x0, waiting for transfers between devices: 12.7 us -> none  [from_partner(): return lax.ppermute(value, 'head', pairs)]
    concatenate x2 -> x0, other arithmetic: 9.15 us -> none  [the longest x1 8.16 us: on_device(): sums = jnp.concatenate([dk, dv], axis=1)]
    unnamed x0 -> x10, local copies, waits for them, and re-layouts: none -> 5.17 us
    ppermute x2 -> x0, starting transfers between devices: 4.67 us -> none  [from_partner(): return lax.ppermute(value, 'head', pairs)]
    slice x1 -> x0, local copies, waits for them, and re-layouts: 4.47 us -> none  [on_device(): gathered[:, pair_width:]]
  transfers between devices with their start and end apart: 4 -> 0, of which waited for: 4 -> 0; matrix products, arithmetic and copies ran while one was open for 0% -> 0% of each run, Pallas kernels for 0% -> 0%
where the time goes in v2:
time: 124 us; the launch traced here: 123 us
  Pallas kernels  118 us (95%)
  local copies, waits for them, and re-layouts  5.17 us (4%)
    pallas_call x1, Pallas kernels, layer(): pl.pallas_call(functools.partial(layer_kernel, bits, sharing), out_shape=...  118 us
    unnamed x10, local copies, waits for them, and re-layouts  5.17 us

profile of v2, /device:TPU:0, one launch (start us, length us, event | category | flops | bytes accessed | tf_op | source)
XLA Modules:
  0.0 123.4 jit_solution(16320516241087590894)
XLA Ops:
  0.6 117.5 %layer.1 = (bf16[128,4096]{1,0:T(8,128)(2,1)}, f32[128,4096]{1,0:T(8,128)}, f32[128,512]{1,0:T(8,128)}, f32[128,512]{1,0:T(8,128)}) custom-call(bf16[128,4096]{1,0:T(8,128)(2,1)} %bitcast.9, bf16[128,4096]{1,0:T(8,128)(2,1)} %bitcast.10, bf16[128,512]{1,0:T(8,128)(2,1)} %bitcast.14, bf16[128,512]{1,0:T(8,128)(2,1)} %bitcast.15), custom_call_target="tpu_custom_call" | custom-call | tf_op jit(solution)/shard_map/layer/pallas_call | solution.py:372
  118.2 0.0 copy-start
  118.2 2.4 %copy.12 = bf16[1,128,4096]{2,1,0:T(8,128)(2,1)} copy(bf16[1,128,4096]{2,1,0:T(8,128)(2,1)} %bitcast.11) | data formatting | bytes 2097152
  120.6 0.0 copy-done
  120.6 0.0 copy-start.2
  120.6 0.0 copy-start.1
  120.6 1.3 %copy.13 = f32[1,128,4096]{2,1,0:T(8,128)} copy(f32[1,128,4096]{2,1,0:T(8,128)S(1)} %bitcast.8) | data formatting | bytes 4194304
  121.9 0.0 copy-done.2
  121.9 0.7 copy.14
  122.6 0.0 copy-done.1
  122.6 0.7 copy.15
Async XLA Ops:
  118.2 2.4 %copy-start = (f32[128,4096]{1,0:T(8,128)S(1)}, f32[128,4096]{1,0:T(8,128)}, u32[]{:S(2)}) copy-start(f32[128,4096]{1,0:T(8,128)} %get-tuple-element.9) | copy-start | bytes 6291460
  120.6 1.3 %copy-start.2 = (f32[128,512]{1,0:T(8,128)S(1)}, f32[128,512]{1,0:T(8,128)}, u32[]{:S(2)}) copy-start(f32[128,512]{1,0:T(8,128)} %get-tuple-element.10) | copy-start | bytes 786436
  120.6 2.0 %copy-start.1 = (f32[128,512]{1,0:T(8,128)S(1)}, f32[128,512]{1,0:T(8,128)}, u32[]{:S(2)}) copy-start(f32[128,512]{1,0:T(8,128)} %get-tuple-element.11) | copy-start | bytes 786436
